TPU v7x, 32 devices: a whole 2x2x4 slice. The times are simulated.
32 devices in a mesh: tbl: 8 (over z, y), pair: 4 (over x, core).
Axes of the slice: x: 2, y: 2, z: 4, core: 2. Of those that a mesh axis runs over, the one named last changes fastest.
Arguments:
- codes: bfloat16 [112, 64, 16384], P('tbl', None, 'pair'), may hold values from -127 to 127
- scales: float32 [112, 16384], P('tbl', 'pair'), may hold values from 0.002 to 0.02
- shard_slot: int32 [8, 14], replicated, may hold values from -1 to 53, as said below
- weight_first: bfloat16 [351, 1024], replicated, may hold values from -0.3125 to 0.3125
- bias_first: float32 [1024], replicated, may hold values from -3 to 3
- weight_second: bfloat16 [1024, 1024], replicated, may hold values from -0.1875 to 0.1875
- bias_second: float32 [1024], replicated, may hold values from -3 to 3
- weight_third: bfloat16 [1024, 512], replicated, may hold values from -0.1875 to 0.1875
- bias_third: float32 [512], replicated, may hold values from -3 to 3
- weight_fourth: bfloat16 [512, 256], replicated, may hold values from -0.25 to 0.25
- bias_fourth: float32 [256], replicated, may hold values from -3 to 3
- weight_out: bfloat16 [256], replicated, may hold values from -0.375 to 0.375
- bias_out: float32 [1], replicated, may hold values from -3 to 3
Outputs:
- logits: float32 [4, 4096], P(None, 'tbl')
Inputs may be any that keep to these rules, and one draw needn't show every extreme that they name: `shard_slot`: each shard 0 to 53 stands in exactly one slot; all other slots hold -1. For k below half of the tbl size, row k holds its shards in its first slots and the row half the tbl size further holds its shards in its last slots, and the two rows hold 14 shards or fewer together. Some row holds 14 shards.
All inputs are finite; a program needn't handle non-finite values.
Results may differ from a plain program's by a relative error of at most 0.03.
Values may be sent and summed in bfloat16 or wider, within the bound.
No kernel may reach another device: no remote copies, remote signals or barrier semaphores. Data moves between devices by JAX's collectives and lax.ppermute only.
A program may use at most 128 MiB of HBM per device.

v0:
```python
import jax
import jax.numpy as jnp
import numpy as np
from jax import lax
from jax.sharding import PartitionSpec as P

TABLES = 27


def pair_columns(tables):
    first, second = np.triu_indices(tables, 1)
    return (first * tables + second).astype(np.int32)


def shard_positions(slot_table, shard_total):
    flat = slot_table.reshape(-1)
    matches = flat[None, :] == jnp.arange(shard_total, dtype=jnp.int32)[:, None]
    places = jnp.arange(flat.shape[0], dtype=jnp.int32)[None, :]
    return jnp.sum(jnp.where(matches, places, 0), axis=1)


def dense_layer(inputs, weight, bias):
    product = jnp.dot(
        inputs.astype(jnp.float32), weight.astype(jnp.float32), precision=lax.Precision.HIGHEST
    )
    return jax.nn.relu(product + bias).astype(jnp.bfloat16)


def score_samples(picked_codes, picked_scales, layers):
    table_count = picked_codes.shape[0] // 2
    column_count = picked_codes.shape[1]
    count = picked_codes.shape[2]
    halves = picked_codes.reshape(table_count, 2, column_count, count)
    half_scales = picked_scales.reshape(table_count, 2, count)
    gram = jnp.zeros((count, table_count, table_count), jnp.float32)
    for part_index in range(2):
        block_codes = halves[:, part_index].astype(jnp.float32)
        products = jnp.einsum(
            "icb,jcb->bij", block_codes, block_codes, precision=lax.Precision.HIGHEST
        )
        factor = half_scales[:, part_index]
        outer = jnp.transpose(factor)[:, :, None] * jnp.transpose(factor)[:, None, :]
        gram = gram + products * outer
    flat = gram.reshape(count, table_count * table_count)
    hidden = flat[:, pair_columns(table_count)].astype(jnp.bfloat16)
    for weight, bias in layers[:-1]:
        hidden = dense_layer(hidden, weight, bias)
    weight_last, bias_last = layers[-1]
    final = jnp.dot(
        hidden.astype(jnp.float32), weight_last.astype(jnp.float32), precision=lax.Precision.HIGHEST
    )
    return final + bias_last[0]


def per_device(
    codes,
    scales,
    shard_slot,
    weight_first,
    bias_first,
    weight_second,
    bias_second,
    weight_third,
    bias_third,
    weight_fourth,
    bias_fourth,
    weight_out,
    bias_out,
):
    layers = (
        (weight_first, bias_first),
        (weight_second, bias_second),
        (weight_third, bias_third),
        (weight_fourth, bias_fourth),
        (weight_out, bias_out),
    )
    slot_count = codes.shape[0]
    column_count = codes.shape[1]
    tbl_count = lax.axis_size("tbl")
    batch_local = codes.shape[2] // tbl_count
    shard_total = 2 * TABLES

    def make_scorer(positions):

        def scorer(received):
            got_codes, got_scales = received
            picked_codes = jnp.take(got_codes[:, :, 0, :], positions, axis=0)
            picked_scales = jnp.take(got_scales[:, 0, 0, :], positions, axis=0)
            return score_samples(picked_codes, picked_scales, layers)

        return scorer

    packed_codes = codes.reshape(slot_count, column_count, tbl_count, batch_local)
    packed_scales = scales.reshape(slot_count, 1, tbl_count, batch_local)
    scorer = make_scorer(shard_positions(shard_slot, shard_total))
    logits = scorer(
        (
            lax.all_to_all(packed_codes, "tbl", split_axis=2, concat_axis=0, tiled=True),
            lax.all_to_all(
                packed_scales.astype(jnp.bfloat16), "tbl", split_axis=2, concat_axis=0, tiled=True
            ).astype(packed_scales.dtype),
        )
    )
    return lax.all_gather(logits[None, :], "pair", axis=0, tiled=True)


def solution(mesh):
    return jax.shard_map(
        per_device,
        mesh=mesh,
        in_specs=(
            P("tbl", None, "pair"),
            P("tbl", "pair"),
            P(),
            P(),
            P(),
            P(),
            P(),
            P(),
            P(),
            P(),
            P(),
            P(),
            P(),
        ),
        out_specs=P(None, "tbl"),
        check_vma=False,
    )
```

profile of v0, /device:TPU:0, one launch (start us, length us, event | category | flops | bytes accessed | tf_op | source)
XLA Modules:
  0.0 243.0 jit_solution(14735998043598674516)
XLA Ops:
  0.0 0.0 copy-start
  0.0 1.1 convert_element_type.56
  1.2 0.7 copy.51
  1.9 7.3 %all-to-all-start.1 = ((bf16[14,1,8,512]{3,0,1,2:T(8,128)(2,1)}), bf16[14,1,8,512]{3,0,1,2:T(8,128)(2,1)S(1)}, u32[]{:S(2)}, u32[]{:S(2)}) async-start(bf16[14,1,8,512]{3,0,1,2:T(8,128)(2,1)} %copy.51), calls=%async_computation.1 | async-start | bytes 262144 | tf_op jit(solution)/shard_map/all_to_all | solution.py:99
  9.2 7.2 %copy.60 = bf16[14,8,8,8,512]{4,3,1,0,2:T(8,128)(2,1)} copy(bf16[14,8,8,8,512]{4,3,2,1,0:T(8,128)(2,1)} %bitcast.62) | data formatting | bytes 14680064 | tf_op jit(solution)/shard_map/reshape | solution.py:93
  16.4 0.1 all-to-all-done.1
  16.5 0.0 copy-start.2
  16.5 0.0 copy-start.10
  16.5 0.0 copy-start.3
  16.5 6.0 %all-to-all-start = ((bf16[14,64,8,512]{3,1,0,2:T(8,128)(2,1)}), bf16[14,64,8,512]{3,1,0,2:T(8,128)(2,1)}, u32[]{:S(2)}, u32[]{:S(2)}) async-start(bf16[14,64,8,512]{3,1,0,2:T(8,128)(2,1)} %bitcast.60), calls=%async_computation | async-start | bytes 14680064 | tf_op jit(solution)/shard_map/all_to_all | solution.py:98
  22.6 0.0 copy-done.2
  22.6 0.1 eq.15
  22.6 0.1 select_reduce_fusion
  22.8 0.1 reduce_sum.14
  22.9 0.1 copy.47
  23.0 0.0 copy-done.10
  23.7 0.0 copy-done.3
  23.8 0.6 gather_fusion.1
  24.4 0.1 gather.18
  24.5 0.2 copy.52
  24.8 157.9 %all-to-all-done = bf16[14,64,8,512]{3,1,0,2:T(8,128)(2,1)} async-done(((bf16[14,64,8,512]{3,1,0,2:T(8,128)(2,1)}), bf16[14,64,8,512]{3,1,0,2:T(8,128)(2,1)}, u32[]{:S(2)}, u32[]{:S(2)}) %all-to-all-start) | async-done | bytes 7340064 | tf_op jit(solution)/shard_map/all_to_all | solution.py:98
  182.7 5.7 %gather_fusion = bf16[54,64,512]{2,1,0:T(8,128)(2,1)} fusion(bf16[112,64,512]{2,1,0:T(8,128)(2,1)} %bitcast.2, s32[1024]{0:T(1024)S(1)} %pad_clamp_fusion.1), kind=kCustom, calls=%fused_computation | custom fusion | bytes 7078104 | tf_op jit(solution)/shard_map/jit(_take)/gather | solution.py:87
  188.4 13.0 %copy.49 = bf16[27,2,64,512]{2,0,3,1:T(8,128)(2,1)} copy(bf16[27,2,64,512]{3,2,1,0:T(8,128)(2,1)} %bitcast.61) | data formatting | bytes 7077888 | tf_op jit(solution)/shard_map/jit(_take)/gather | solution.py:87
  201.5 7.4 %broadcast_select_fusion = bf16[27,2,64,512]{2,0,3,1:T(8,128)(2,1)} fusion(bf16[27,2,64,512]{2,0,3,1:T(8,128)(2,1)} %copy.49, pred[27,2]{0,1:T(4,128)(4,1)S(1)} %copy.47), kind=kLoop, calls=%fused_computation.4 | loop fusion | flops 1769472 | bytes 7077942 | tf_op jit(solution)/shard_map/jit(_take)/select_n | solution.py:87
  208.9 0.0 copy-start.1
  208.9 5.9 %fusion = f32[512,27,27]{2,1,0:T(8,128)S(1)} fusion(bf16[27,2,64,512]{2,0,3,1:T(8,128)(2,1)} %broadcast_select_fusion), kind=kOutput, calls=%fused_computation.7 | convolution fusion | flops 47775744 | bytes 5687296 | tf_op jit(solution)/shard_map/icb,jcb->bij/dot_general | solution.py:38
  214.7 0.0 copy-done.1
  214.7 6.7 %multiply_add_fusion = bf16[512,27,27]{2,1,0:T(8,128)(2,1)} fusion(f32[512,27,27]{2,1,0:T(8,128)S(1)} %fusion, f32[512,27]{1,0:T(8,128)S(1)} %get-tuple-element.6, f32[512,27]{1,0:T(8,128)S(1)} %get-tuple-element.5, bf16[27,2,64,512]{2,0,3,1:T(8,128)(2,1)S(1)} %copy-done.1), kind=kOutput, calls=%fused_computation.3 | convolution fusion | flops 50015232 | bytes 14377984 | tf_op jit(solution)/shard_map/icb,jcb->bij/dot_general | solution.py:38
  221.5 0.0 copy-start.6
  221.5 0.0 copy-start.7
  221.5 7.7 %reshape.100 = bf16[512,729]{1,0:T(8,128)(2,1)} reshape(bf16[512,27,27]{2,1,0:T(8,128)(2,1)} %multiply_add_fusion) | data formatting | bytes 1492992 | tf_op jit(solution)/shard_map/reshape | solution.py:44
  229.2 1.4 copy.54
  230.6 0.0 copy-start.8
  230.6 2.0 gather_fusion.2
  232.7 0.0 copy-done.6
  232.7 0.0 copy-start.4
  232.7 0.0 copy-start.5
  232.7 0.0 copy-start.9
  232.7 1.9 maximum_convert_fusion.1
  234.7 0.0 copy-done
  234.7 0.0 copy-done.7
  234.7 1.3 maximum_convert_fusion
  236.0 0.0 copy-done.8
  236.0 0.0 copy-done.4
  236.0 0.7 fusion.3
  236.7 0.0 copy-done.5
  236.7 0.0 copy-done.9
  236.7 0.3 fusion.5
  237.0 0.2 fusion.8
  237.2 5.2 %all-gather.1 = f32[4,1,512]{2,1,0:T(1,128)S(1)} all-gather(f32[1,1,512]{2,1,0:T(1,128)S(1)} %bitcast.66), channel_id=2, replica_groups=mesh['tbl'=8,'pair'=4] {'pair'}, dimensions={0}, use_global_device_ids=true | all-gather | bytes 10240 | tf_op jit(solution)/shard_map/all_gather | solution.py:104
  242.4 0.6 copy.61
  (12 shorter events, 0.2 us)
Async XLA Ops:
  0.0 234.7 %copy-start = (bf16[1024,1024]{1,0:T(8,128)(2,1)S(1)}, bf16[1024,1024]{1,0:T(8,128)(2,1)}, u32[]{:S(2)}) copy-start(bf16[1024,1024]{1,0:T(8,128)(2,1)} %param.20) | copy-start | bytes 6291460
  1.9 14.7 %all-to-all-start.1 = ((bf16[14,1,8,512]{3,0,1,2:T(8,128)(2,1)}), bf16[14,1,8,512]{3,0,1,2:T(8,128)(2,1)S(1)}, u32[]{:S(2)}, u32[]{:S(2)}) async-start(bf16[14,1,8,512]{3,0,1,2:T(8,128)(2,1)} %copy.51), calls=%async_computation.1 | async-start | bytes 262144 | tf_op jit(solution)/shard_map/all_to_all | solution.py:99
  16.5 6.0 %copy-start.2 = (s32[8,14]{1,0:T(8,128)S(1)}, s32[8,14]{1,0:T(8,128)}, u32[]{:S(2)}) copy-start(s32[8,14]{1,0:T(8,128)} %param.17) | copy-start | bytes 1348
  16.5 6.5 %copy-start.10 = (bf16[256]{0:T(256)(128)(2,1)S(1)}, bf16[256]{0:T(256)(128)(2,1)}, u32[]{:S(2)}) copy-start(bf16[256]{0:T(256)(128)(2,1)} %param.26) | copy-start | bytes 1540
  16.5 7.1 %copy-start.3 = (s32[351]{0:T(512)S(1)}, s32[351]{0:T(512)}, u32[]{:S(2)}) copy-start(s32[351]{0:T(512)} %constant.49) | copy-start | bytes 4216
  16.5 166.2 %all-to-all-start = ((bf16[14,64,8,512]{3,1,0,2:T(8,128)(2,1)}), bf16[14,64,8,512]{3,1,0,2:T(8,128)(2,1)}, u32[]{:S(2)}, u32[]{:S(2)}) async-start(bf16[14,64,8,512]{3,1,0,2:T(8,128)(2,1)} %bitcast.60), calls=%async_computation | async-start | bytes 14680064 | tf_op jit(solution)/shard_map/all_to_all | solution.py:98
  208.9 5.9 %copy-start.1 = (bf16[27,2,64,512]{2,0,3,1:T(8,128)(2,1)S(1)}, bf16[27,2,64,512]{2,0,3,1:T(8,128)(2,1)}, u32[]{:S(2)}) copy-start(bf16[27,2,64,512]{2,0,3,1:T(8,128)(2,1)} %broadcast_select_fusion) | copy-start | bytes 10616836
  221.5 11.2 %copy-start.6 = (f32[1024]{0:T(1024)S(1)}, f32[1024]{0:T(1024)}, u32[]{:S(2)}) copy-start(f32[1024]{0:T(1024)} %param.19) | copy-start | bytes 12292
  221.5 13.2 %copy-start.7 = (f32[1024]{0:T(1024)S(1)}, f32[1024]{0:T(1024)}, u32[]{:S(2)}) copy-start(f32[1024]{0:T(1024)} %param.21) | copy-start | bytes 12292
  230.6 5.4 %copy-start.8 = (f32[512]{0:T(512)S(1)}, f32[512]{0:T(512)}, u32[]{:S(2)}) copy-start(f32[512]{0:T(512)} %param.23) | copy-start | bytes 6148
  232.7 3.3 %copy-start.4 = (bf16[1024,512]{1,0:T(8,128)(2,1)S(1)}, bf16[1024,512]{1,0:T(8,128)(2,1)}, u32[]{:S(2)}) copy-start(bf16[1024,512]{1,0:T(8,128)(2,1)} %param.22) | copy-start | bytes 3145732
  232.7 4.0 %copy-start.5 = (bf16[512,256]{1,0:T(8,128)(2,1)S(1)}, bf16[512,256]{1,0:T(8,128)(2,1)}, u32[]{:S(2)}) copy-start(bf16[512,256]{1,0:T(8,128)(2,1)} %param.24) | copy-start | bytes 786436
  232.7 4.0 %copy-start.9 = (f32[256]{0:T(256)S(1)}, f32[256]{0:T(256)}, u32[]{:S(2)}) copy-start(f32[256]{0:T(256)} %param.25) | copy-start | bytes 3076
where the time goes:
time: 244 us; the launch traced here: 243 us
  waiting for transfers between devices  158 us (65%)
  local copies, waits for them, and re-layouts  39.8 us (16%)
  matrix products  17 us (7%)
  starting transfers between devices  13.3 us (5%)
  other arithmetic  8.71 us (4%)
  blocking collectives  5.2 us (2%)
    all_to_all x1, waiting for transfers between devices, per_device(): lax.all_to_all(packed_codes, 'tbl', split_axis=2, concat_axis=0, tiled=True)  158 us
    gather x2, local copies, waits for them, and re-layouts, scorer(): picked_codes = jnp.take(got_codes[:, :, 0, :], positions, axis=0)  18.8 us
    dot_general x2, matrix products, score_samples(): jnp.einsum('icb,jcb->bij', block_codes, block_codes, precision=lax.Precis...  12.6 us
    reshape x2, local copies, waits for them, and re-layouts, score_samples(): flat = gram.reshape(count, table_count * table_count)  9.12 us
    select_n x2, other arithmetic, scorer(): picked_codes = jnp.take(got_codes[:, :, 0, :], positions, axis=0)  7.4 us
    all_to_all x1, starting transfers between devices, per_device(): lax.all_to_all(packed_scales.astype(jnp.bfloat16), 'tbl', split_axis=2, c...  7.31 us
    reshape x1, local copies, waits for them, and re-layouts, per_device(): codes.reshape(slot_count, column_count, tbl_count, batch_local)  7.22 us
    all_to_all x1, starting transfers between devices, per_device(): lax.all_to_all(packed_codes, 'tbl', split_axis=2, concat_axis=0, tiled=True)  6.03 us
  transfers between devices with their start and end apart: 2, of which 2 were waited for; matrix products, arithmetic and copies ran while one was open for 4% of the time, Pallas kernels for 0%

commit v1 on v0

--- a/solution.py
+++ b/solution.py
@@ -95,7 +95,12 @@
     scorer = make_scorer(shard_positions(shard_slot, shard_total))
     logits = scorer(
         (
-            lax.all_to_all(packed_codes, "tbl", split_axis=2, concat_axis=0, tiled=True),
+            jnp.concatenate(
+                lax.all_to_all(
+                    jnp.stack(jnp.split(packed_codes, lax.axis_size("tbl"), axis=2)), "tbl", 0, 0
+                ),
+                axis=0,
+            ),
             lax.all_to_all(
                 packed_scales.astype(jnp.bfloat16), "tbl", split_axis=2, concat_axis=0, tiled=True
             ).astype(packed_scales.dtype),

time: 244 us -> 271 us (1.11)
  local copies, waits for them, and re-layouts: 39.8 us -> 67.5 us
    unnamed x25 -> x39, local copies, waits for them, and re-layouts: 0.7 us -> 20.4 us
    split x0 -> x1, local copies, waits for them, and re-layouts: none -> 14 us  [per_device(): jnp.split(packed_codes, lax.axis_size('tbl'), axis=2)]
    reshape x1 -> x0, local copies, waits for them, and re-layouts: 7.22 us -> none  [per_device(): codes.reshape(slot_count, column_count, tbl_count, batch_local)]
  transfers between devices with their start and end apart: 2 -> 2, of which waited for: 2 -> 1; matrix products, arithmetic and copies ran while one was open for 4% -> 13% of each run, Pallas kernels for 0% -> 0%
where the time goes in v1:
time: 271 us
  waiting for transfers between devices  158 us (58%)
  local copies, waits for them, and re-layouts  67.5 us (25%)
  matrix products  17 us (6%)
  starting transfers between devices  13.5 us (5%)
  other arithmetic  8.71 us (3%)
  blocking collectives  5.2 us (2%)
    all_to_all x1, waiting for transfers between devices, per_device(): lax.all_to_all(jnp.stack(jnp.split(packed_codes, lax.axis_size('tbl'), ax...  158 us
    unnamed x39, local copies, waits for them, and re-layouts  20.4 us
    gather x2, local copies, waits for them, and re-layouts, scorer(): picked_codes = jnp.take(got_codes[:, :, 0, :], positions, axis=0)  18.7 us
    split x1, local copies, waits for them, and re-layouts, per_device(): jnp.split(packed_codes, lax.axis_size('tbl'), axis=2)  14 us
    dot_general x2, matrix products, score_samples(): jnp.einsum('icb,jcb->bij', block_codes, block_codes, precision=lax.Precis...  12.6 us
    reshape x2, local copies, waits for them, and re-layouts, score_samples(): flat = gram.reshape(count, table_count * table_count)  9.11 us
    select_n x2, other arithmetic, scorer(): picked_codes = jnp.take(got_codes[:, :, 0, :], positions, axis=0)  7.4 us
    all_to_all x1, starting transfers between devices, per_device(): lax.all_to_all(packed_scales.astype(jnp.bfloat16), 'tbl', split_axis=2, c...  7.31 us
  transfers between devices with their start and end apart: 2, of which 1 were waited for; matrix products, arithmetic and copies ran while one was open for 13% of the time, Pallas kernels for 0%

profile of v1, /device:TPU:0, one launch (start us, length us, event | category | flops | bytes accessed | tf_op | source)
XLA Modules:
  0.0 270.7 jit_solution(3295822728417463317)
XLA Ops:
  0.0 0.0 copy-start
  0.0 1.1 convert_element_type.56
  1.2 0.7 copy.117
  1.9 7.3 %all-to-all-start.1 = ((bf16[14,1,8,512]{3,0,1,2:T(8,128)(2,1)}), bf16[14,1,8,512]{3,0,1,2:T(8,128)(2,1)S(1)}, u32[]{:S(2)}, u32[]{:S(2)}) async-start(bf16[14,1,8,512]{3,0,1,2:T(8,128)(2,1)} %copy.117), calls=%async_computation.1 | async-start | bytes 262144 | tf_op jit(solution)/shard_map/all_to_all | solution.py:104
  9.2 8.0 %copy.130 = bf16[112,8,8,512]{3,2,1,0:T(8,128)(2,1)S(1)} copy(bf16[112,8,8,512]{3,1,2,0:T(8,128)(2,1)} %bitcast.74) | data formatting | bytes 14680064
  17.2 14.0 %fusion.8 = (bf16[14,64,1,512]{3,2,1,0:T(2,128)(2,1)S(1)}, bf16[14,64,1,512]{3,2,1,0:T(2,128)(2,1)S(1)}, bf16[14,64,1,512]{3,2,1,0:T(2,128)(2,1)}, bf16[14,64,1,...) fusion(bf16[14,64,8,512]{3,2,1,0:T(8,128)(2,1)S(1)} %bitcast.72), kind=kLoop, calls=%fused_computation.41 | loop fusion | bytes 14680064 | tf_op jit(solution)/shard_map/split | solution.py:100
  31.2 0.0 copy-start.4
  31.2 0.0 copy-start.3
  31.2 0.0 copy-start.2
  31.2 2.8 %bitcast_dynamic-update-slice_fusion.7 = bf16[8,14,64,1,512]{4,2,1,3,0:T(8,128)(2,1)} fusion(bf16[14,64,1,512]{3,2,1,0:T(2,128)(2,1)} %get-tuple-element.12), kind=kLoop, calls=%fused_computation.24 | loop fusion | bytes 1835008
  34.0 2.8 %bitcast_dynamic-update-slice_fusion.6 = bf16[8,14,64,1,512]{4,2,1,3,0:T(8,128)(2,1)} fusion(bf16[8,14,64,1,512]{4,2,1,3,0:T(8,128)(2,1)} %bitcast_dynamic-update-slice_fusion.7, bf16[14,64,1,512]{3,2,1,0:T(2,128)(2,1)} %get-tuple-element.11), kind=kLoop, calls=%fused_computation.23 | loop fusion | bytes 2752512
  36.8 1.2 bitcast_dynamic-update-slice_fusion.5
  38.0 0.0 copy-done.4
  38.0 1.2 bitcast_dynamic-update-slice_fusion.4
  39.2 0.0 copy-done.3
  39.2 1.2 bitcast_dynamic-update-slice_fusion.3
  40.4 0.0 copy-done.2
  40.4 1.2 bitcast_dynamic-update-slice_fusion.2
  41.7 1.2 bitcast_dynamic-update-slice_fusion.1
  42.9 1.2 bitcast_dynamic-update-slice_fusion
  44.1 0.0 copy-start.13
  44.1 0.0 copy-start.6
  44.1 0.0 all-to-all-done.1
  44.1 6.1 %all-to-all-start = ((bf16[8,14,64,1,512]{4,2,1,3,0:T(8,128)(2,1)}), bf16[8,14,64,1,512]{4,2,1,3,0:T(8,128)(2,1)}, u32[]{:S(2)}, u32[]{:S(2)}) async-start(bf16[8,14,64,1,512]{4,2,1,3,0:T(8,128)(2,1)} %bitcast_dynamic-update-slice_fusion), calls=%async_computation | async-start | bytes 14680064 | tf_op jit(solution)/shard_map/all_to_all | solution.py:99
  50.2 0.0 copy-done.5
  50.3 0.1 eq.15
  50.3 0.1 select_reduce_fusion
  50.4 0.1 reduce_sum.14
  50.6 0.1 copy.114
  50.7 0.0 copy-done.13
  51.4 0.0 copy-done.6
  51.5 0.6 gather_fusion.1
  52.1 0.1 gather.18
  52.2 0.2 copy.118
  52.5 157.9 %all-to-all-done = bf16[8,14,64,1,512]{4,2,1,3,0:T(8,128)(2,1)} async-done(((bf16[8,14,64,1,512]{4,2,1,3,0:T(8,128)(2,1)}), bf16[8,14,64,1,512]{4,2,1,3,0:T(8,128)(2,1)}, u32[]{:S(2)}, u32[]{:S(2)}) %all-to-all-start) | async-done | bytes 7340064 | tf_op jit(solution)/shard_map/all_to_all | solution.py:99
  210.4 5.7 %gather_fusion = bf16[54,64,512]{2,1,0:T(8,128)(2,1)} fusion(bf16[112,64,512]{2,1,0:T(8,128)(2,1)} %bitcast, s32[1024]{0:T(1024)S(1)} %pad_clamp_fusion.1), kind=kCustom, calls=%fused_computation | custom fusion | bytes 7078104 | tf_op jit(solution)/shard_map/jit(_take)/gather | solution.py:87
  216.1 13.1 %copy.115 = bf16[27,2,64,512]{2,0,3,1:T(8,128)(2,1)} copy(bf16[27,2,64,512]{3,2,1,0:T(8,128)(2,1)} %bitcast.73) | data formatting | bytes 7077888 | tf_op jit(solution)/shard_map/jit(_take)/gather | solution.py:87
  229.1 7.4 %broadcast_select_fusion = bf16[27,2,64,512]{2,0,3,1:T(8,128)(2,1)} fusion(bf16[27,2,64,512]{2,0,3,1:T(8,128)(2,1)} %copy.115, pred[27,2]{0,1:T(4,128)(4,1)S(1)} %copy.114), kind=kLoop, calls=%fused_computation.4 | loop fusion | flops 1769472 | bytes 7077942 | tf_op jit(solution)/shard_map/jit(_take)/select_n | solution.py:87
  236.5 0.0 copy-start.1
  236.5 5.9 %fusion = f32[512,27,27]{2,1,0:T(8,128)S(1)} fusion(bf16[27,2,64,512]{2,0,3,1:T(8,128)(2,1)} %broadcast_select_fusion), kind=kOutput, calls=%fused_computation.6 | convolution fusion | flops 47775744 | bytes 5687296 | tf_op jit(solution)/shard_map/icb,jcb->bij/dot_general | solution.py:38
  242.4 0.0 copy-done.1
  242.4 6.8 %multiply_add_fusion = bf16[512,27,27]{2,1,0:T(8,128)(2,1)} fusion(f32[512,27,27]{2,1,0:T(8,128)S(1)} %fusion, f32[512,27]{1,0:T(8,128)S(1)} %get-tuple-element.14, f32[512,27]{1,0:T(8,128)S(1)} %get-tuple-element.13, bf16[27,2,64,512]{2,0,3,1:T(8,128)(2,1)S(1)} %copy-done.1), kind=kOutput, calls=%fused_computation.3 | convolution fusion | flops 50015232 | bytes 14377984 | tf_op jit(solution)/shard_map/icb,jcb->bij/dot_general | solution.py:38
  249.2 0.0 copy-start.9
  249.2 7.7 %reshape.99 = bf16[512,729]{1,0:T(8,128)(2,1)} reshape(bf16[512,27,27]{2,1,0:T(8,128)(2,1)} %multiply_add_fusion) | data formatting | bytes 1492992 | tf_op jit(solution)/shard_map/reshape | solution.py:44
  256.9 1.4 copy.120
  258.3 0.0 copy-start.11
  258.3 2.0 gather_fusion.2
  260.4 0.0 copy-done.9
  260.4 0.0 copy-start.7
  260.4 0.0 copy-start.8
  260.4 0.0 copy-start.12
  260.4 1.9 maximum_convert_fusion.1
  262.4 0.0 copy-done
  262.4 0.0 copy-done.10
  262.4 1.3 maximum_convert_fusion
  263.6 0.0 copy-done.11
  263.7 0.0 copy-done.7
  263.7 0.7 fusion.3
  264.4 0.0 copy-done.8
  264.4 0.0 copy-done.12
  264.4 0.3 fusion.5
  264.7 0.2 fusion.9
  264.9 5.2 %all-gather.1 = f32[4,1,512]{2,1,0:T(1,128)S(1)} all-gather(f32[1,1,512]{2,1,0:T(1,128)S(1)} %bitcast.78), channel_id=2, replica_groups=mesh['tbl'=8,'pair'=4] {'pair'}, dimensions={0}, use_global_device_ids=true | all-gather | bytes 10240 | tf_op jit(solution)/shard_map/all_gather | solution.py:109
  270.1 0.6 copy.141
  (14 shorter events, 0.2 us)
Async XLA Ops:
  0.0 262.4 %copy-start = (bf16[1024,1024]{1,0:T(8,128)(2,1)S(1)}, bf16[1024,1024]{1,0:T(8,128)(2,1)}, u32[]{:S(2)}) copy-start(bf16[1024,1024]{1,0:T(8,128)(2,1)} %param.20) | copy-start | bytes 6291460
  1.9 42.2 %all-to-all-start.1 = ((bf16[14,1,8,512]{3,0,1,2:T(8,128)(2,1)}), bf16[14,1,8,512]{3,0,1,2:T(8,128)(2,1)S(1)}, u32[]{:S(2)}, u32[]{:S(2)}) async-start(bf16[14,1,8,512]{3,0,1,2:T(8,128)(2,1)} %copy.117), calls=%async_computation.1 | async-start | bytes 262144 | tf_op jit(solution)/shard_map/all_to_all | solution.py:104
  31.2 6.8 %copy-start.4 = (bf16[14,64,1,512]{3,2,1,0:T(2,128)(2,1)S(1)}, bf16[14,64,1,512]{3,2,1,0:T(2,128)(2,1)}, u32[]{:S(2)}) copy-start(bf16[14,64,1,512]{3,2,1,0:T(2,128)(2,1)} %get-tuple-element.9) | copy-start | bytes 2752516
  31.2 8.0 %copy-start.3 = (bf16[14,64,1,512]{3,2,1,0:T(2,128)(2,1)S(1)}, bf16[14,64,1,512]{3,2,1,0:T(2,128)(2,1)}, u32[]{:S(2)}) copy-start(bf16[14,64,1,512]{3,2,1,0:T(2,128)(2,1)} %get-tuple-element.8) | copy-start | bytes 2752516
  31.2 9.2 %copy-start.2 = (bf16[14,64,1,512]{3,2,1,0:T(2,128)(2,1)S(1)}, bf16[14,64,1,512]{3,2,1,0:T(2,128)(2,1)}, u32[]{:S(2)}) copy-start(bf16[14,64,1,512]{3,2,1,0:T(2,128)(2,1)} %get-tuple-element.7) | copy-start | bytes 2752516
  44.1 6.2 %copy-start.5 = (s32[8,14]{1,0:T(8,128)S(1)}, s32[8,14]{1,0:T(8,128)}, u32[]{:S(2)}) copy-start(s32[8,14]{1,0:T(8,128)} %param.17) | copy-start | bytes 1348
  44.1 6.6 %copy-start.13 = (bf16[256]{0:T(256)(128)(2,1)S(1)}, bf16[256]{0:T(256)(128)(2,1)}, u32[]{:S(2)}) copy-start(bf16[256]{0:T(256)(128)(2,1)} %param.26) | copy-start | bytes 1540
  44.1 7.3 %copy-start.6 = (s32[351]{0:T(512)S(1)}, s32[351]{0:T(512)}, u32[]{:S(2)}) copy-start(s32[351]{0:T(512)} %constant.49) | copy-start | bytes 4216
  44.1 166.3 %all-to-all-start = ((bf16[8,14,64,1,512]{4,2,1,3,0:T(8,128)(2,1)}), bf16[8,14,64,1,512]{4,2,1,3,0:T(8,128)(2,1)}, u32[]{:S(2)}, u32[]{:S(2)}) async-start(bf16[8,14,64,1,512]{4,2,1,3,0:T(8,128)(2,1)} %bitcast_dynamic-update-slice_fusion), calls=%async_computation | async-start | bytes 14680064 | tf_op jit(solution)/shard_map/all_to_all | solution.py:99
  236.5 5.9 %copy-start.1 = (bf16[27,2,64,512]{2,0,3,1:T(8,128)(2,1)S(1)}, bf16[27,2,64,512]{2,0,3,1:T(8,128)(2,1)}, u32[]{:S(2)}) copy-start(bf16[27,2,64,512]{2,0,3,1:T(8,128)(2,1)} %broadcast_select_fusion) | copy-start | bytes 10616836
  249.2 11.2 %copy-start.9 = (f32[1024]{0:T(1024)S(1)}, f32[1024]{0:T(1024)}, u32[]{:S(2)}) copy-start(f32[1024]{0:T(1024)} %param.19) | copy-start | bytes 12292
  249.2 13.2 %copy-start.10 = (f32[1024]{0:T(1024)S(1)}, f32[1024]{0:T(1024)}, u32[]{:S(2)}) copy-start(f32[1024]{0:T(1024)} %param.21) | copy-start | bytes 12292
  258.3 5.4 %copy-start.11 = (f32[512]{0:T(512)S(1)}, f32[512]{0:T(512)}, u32[]{:S(2)}) copy-start(f32[512]{0:T(512)} %param.23) | copy-start | bytes 6148
  260.4 3.3 %copy-start.7 = (bf16[1024,512]{1,0:T(8,128)(2,1)S(1)}, bf16[1024,512]{1,0:T(8,128)(2,1)}, u32[]{:S(2)}) copy-start(bf16[1024,512]{1,0:T(8,128)(2,1)} %param.22) | copy-start | bytes 3145732
  260.4 4.0 %copy-start.8 = (bf16[512,256]{1,0:T(8,128)(2,1)S(1)}, bf16[512,256]{1,0:T(8,128)(2,1)}, u32[]{:S(2)}) copy-start(bf16[512,256]{1,0:T(8,128)(2,1)} %param.24) | copy-start | bytes 786436
  260.4 4.0 %copy-start.12 = (f32[256]{0:T(256)S(1)}, f32[256]{0:T(256)}, u32[]{:S(2)}) copy-start(f32[256]{0:T(256)} %param.25) | copy-start | bytes 3076
